TPU v7x, 512 devices: a whole 4x8x8 slice. The times are simulated.
512 devices in a mesh: rep: 32 (over x, y), tp: 16 (over z, core).
Axes of the slice: x: 4, y: 8, z: 8, core: 2. Of those that a mesh axis runs over, the one named last changes fastest.
Arguments:
- queries: bfloat16 [416, 48, 4096], P('rep', None, 'tp'), may hold values from -33 to 33
- tree_cache: bfloat16 [416, 2, 48, 4096], P('rep', None, None, 'tp'), may hold values from -11 to 11
- tree_mask: int32 [416, 48, 48], P('rep'), may hold values from 0 to 1, as said below
- dest_group: int32 [416, 1], P('rep'), may hold values from 0 to 31; in each aligned block of 13 rows (0 to 12, 13 to 25, ...) at most 2 rows name the same one
- accepted_path: int32 [416, 8], P('rep'), may hold values from 0 to 47
- prompt_cache: bfloat16 [32, 2, 152, 4096], P('rep', None, None, 'tp'), may hold values from -11 to 11
- first_len: int32 [32], P('rep'), may hold values from 2 to 152
- spill_cache: bfloat16 [32, 2, 152, 4096], P('rep', None, None, 'tp'), may hold values from -6 to 6
- spill_len: int32 [32], P('rep'), may hold values from 76 to 152
- out_weight: bfloat16 [4096, 4096], P(None, 'tp'), may hold values from -0.09375 to 0.09375
Outputs:
- projected: bfloat16 [416, 48, 4096], P('rep', None, 'tp')
- accepted_cache: bfloat16 [416, 2, 8, 4096], P('rep', None, None, 'tp')
Inputs may be any that keep to these rules, and one draw needn't show every extreme that they name: `dest_group`: in each aligned block of 13 requests (those of one index of rep) no group is named more than 2 times. Row t of tree_mask[r] marks token t and its ancestors in a tree whose parents come before their children.
All inputs are finite; a program needn't handle non-finite values.
Results may differ from a plain program's by a relative error of at most 0.014.
Values may be sent and summed in bfloat16 or wider, within the bound.
A program may use at most 64 MiB of HBM per device.

v0:
```python
import math
import jax
import jax.numpy as jnp
from jax import lax
from jax.sharding import PartitionSpec as P

HD = 128
TREE = 48
PCAP = 152
NEG_FILL = -1e30


def swapped(value, axis, apart):
    mask = 2**apart
    pairs = [(source, source ^ mask) for source in range(lax.axis_size(axis))]
    return lax.ppermute(value, axis, pairs)


def attend_part(query_rows, key_rows, value_rows, visible, head_size):
    heads_here = query_rows.shape[2] // head_size
    maxima = []
    totals = []
    partial_sums = []
    for head_index in range(heads_here):
        lower = head_index * head_size
        upper = lower + head_size
        scores = lax.dot_general(
            query_rows[:, :, lower:upper],
            key_rows[:, :, lower:upper],
            (((2,), (2,)), ((0,), (0,))),
            preferred_element_type=jnp.float32,
        ) * (1.0 / math.sqrt(head_size))
        scores = jnp.where(visible, scores, NEG_FILL)
        peaks = jnp.max(scores, axis=2)
        raw_weights = jnp.where(visible, jnp.exp(scores - peaks[:, :, None]), 0.0)
        maxima.append(peaks)
        totals.append(jnp.sum(raw_weights, axis=2))
        partial_sums.append(
            lax.dot_general(
                raw_weights.astype(jnp.bfloat16),
                value_rows[:, :, lower:upper],
                (((2,), (1,)), ((0,), (0,))),
                preferred_element_type=jnp.float32,
            )
        )
    return (
        jnp.stack(maxima, axis=-1),
        jnp.stack(totals, axis=-1),
        jnp.concatenate(partial_sums, axis=-1),
    )


def combine_parts(first_part, second_part, head_size):
    max_first, total_first, accum_first = first_part
    max_second, total_second, accum_second = second_part
    peaks = jnp.maximum(max_first, max_second)
    factor_first = jnp.exp(max_first - peaks)
    factor_second = jnp.exp(max_second - peaks)
    totals = total_first * factor_first + total_second * factor_second
    full_shape = accum_first.shape
    split_shape = full_shape[:-1] + (full_shape[-1] // head_size, head_size)
    accum = (
        accum_first.reshape(split_shape) * factor_first[..., None]
        + accum_second.reshape(split_shape) * factor_second[..., None]
    )
    return (peaks, totals, accum.reshape(full_shape))


def local(
    queries,
    tree_cache,
    tree_mask,
    dest_group,
    accepted_path,
    prompt_cache,
    first_len,
    spill_cache,
    spill_len,
    out_weight,
):
    req_here = queries.shape[0]
    local_cols = queries.shape[2]
    heads_here = local_cols // HD
    groups = lax.axis_size("rep")
    per_group = max(2, (req_here + groups - 1) // groups)
    n_slots = groups * per_group
    target = dest_group[:, 0]
    same_target = target[:, None] == target[None, :]
    earlier = jnp.arange(req_here)[None, :] < jnp.arange(req_here)[:, None]
    rank_index = jnp.sum(jnp.logical_and(same_target, earlier), axis=1)
    slot_index = target * per_group + rank_index
    selector = (jnp.arange(n_slots, dtype=jnp.int32)[:, None] == slot_index[None, :]).astype(
        jnp.bfloat16
    )
    outbound = jnp.einsum(
        "sr,rtc->stc", selector, queries, preferred_element_type=jnp.float32
    ).astype(jnp.bfloat16)
    outbound = outbound.reshape(groups, per_group, TREE, local_cols)
    inbound = lax.all_to_all(outbound, "rep", split_axis=0, concat_axis=0, tiled=True)
    routed_rows = inbound.reshape(1, n_slots * TREE, local_cols)
    positions = jnp.arange(PCAP, dtype=jnp.int32)
    prompt_seen = (positions < first_len[0])[None, None, :]
    prompt_part = attend_part(routed_rows, prompt_cache[:, 0], prompt_cache[:, 1], prompt_seen, HD)
    live_flag = (positions < spill_len[0]).astype(jnp.bfloat16)
    partner_cache, partner_flag = swapped((spill_cache, live_flag), "rep", 0)
    spill_seen = (partner_flag > 0.5)[None, None, :]
    spill_part = attend_part(routed_rows, partner_cache[:, 0], partner_cache[:, 1], spill_seen, HD)
    merged_max, merged_total, merged_accum = combine_parts(prompt_part, spill_part, HD)
    back_max, back_total, back_accum = (
        lax.all_to_all(
            merged_max.reshape(groups, per_group, TREE, heads_here),
            "rep",
            split_axis=0,
            concat_axis=0,
            tiled=True,
        ),
        lax.all_to_all(
            merged_total.reshape(groups, per_group, TREE, heads_here),
            "rep",
            split_axis=0,
            concat_axis=0,
            tiled=True,
        ),
        lax.all_to_all(
            merged_accum.reshape(groups, per_group, TREE, local_cols),
            "rep",
            split_axis=0,
            concat_axis=0,
            tiled=True,
        ),
    )
    remote_part = (
        jnp.take(back_max.reshape(n_slots, TREE, heads_here), slot_index, axis=0),
        jnp.take(back_total.reshape(n_slots, TREE, heads_here), slot_index, axis=0),
        jnp.take(back_accum.reshape(n_slots, TREE, local_cols), slot_index, axis=0),
    )
    tree_seen = tree_mask == 1
    tree_part = attend_part(queries, tree_cache[:, 0], tree_cache[:, 1], tree_seen, HD)
    final_max, final_total, final_accum = combine_parts(remote_part, tree_part, HD)
    attn = final_accum.reshape(req_here, TREE, heads_here, HD) / final_total[..., None]
    attn = attn.reshape(req_here * TREE, local_cols).astype(jnp.bfloat16)
    summed = jnp.dot(
        lax.all_gather(attn, "tp", axis=1, tiled=True),
        out_weight,
        preferred_element_type=jnp.float32,
    )
    projected = summed.astype(jnp.bfloat16).reshape(req_here, TREE, out_weight.shape[1])
    accepted_cache = jnp.take_along_axis(tree_cache, accepted_path[:, None, :, None], axis=2)
    return (projected, accepted_cache)


def solution(mesh):
    return jax.shard_map(
        local,
        mesh=mesh,
        in_specs=(
            P("rep", None, "tp"),
            P("rep", None, None, "tp"),
            P("rep", None, None),
            P("rep", None),
            P("rep", None),
            P("rep", None, None, "tp"),
            P("rep"),
            P("rep", None, None, "tp"),
            P("rep"),
            P(None, "tp"),
        ),
        out_specs=(P("rep", None, "tp"), P("rep", None, None, "tp")),
        check_vma=False,
    )
```

profile of v0, /device:TPU:1, one launch (start us, length us, event | category | flops | bytes accessed | tf_op | source)
XLA Modules:
  0.0 319.3 jit_solution(14354112950949048452)
XLA Ops:
  7.2 1.0 convert_reduce_fusion
  8.2 1.1 compare_and_fusion.1
  9.3 1.7 convolution_convert_fusion
  11.0 2.0 copy.131
  13.0 10.7 %all-to-all-start = ((bf16[32,2,48,256]{3,2,1,0:T(8,128)(2,1)}), bf16[32,2,48,256]{3,2,1,0:T(8,128)(2,1)}, u32[]{:S(2)}, u32[]{:S(2)}) async-start(bf16[32,2,48,256]{3,2,1,0:T(8,128)(2,1)} %bitcast.162), calls=%async_computation | async-start | bytes 3145728 | tf_op jit(solution)/shard_map/all_to_all | solution.py:99
  23.8 3.1 collective-permute-start.1
  27.5 2.2 collective-permute-start
  30.5 31.8 %collective-permute-done = bf16[152]{0:T(256)(128)(2,1)S(1)} collective-permute-done((bf16[152]{0:T(256)(128)(2,1)S(1)}, bf16[152]{0:T(256)(128)(2,1)S(1)}, u32[]{:S(2)}, u32[]{:S(2)}) %collective-permute-start) | collective-permute-done | bytes 336 | tf_op jit(solution)/shard_map/ppermute | solution.py:16
  62.3 3.1 fusion.59
  65.3 3.1 fusion.60
  68.4 3.1 fusion.57
  71.5 3.0 fusion.58
  74.8 3.8 %fusion.9 = (f32[3072]{0:T(1024)S(1)}, f32[3072]{0:T(1024)S(1)}, bf16[3072,152]{0,1:T(8,128)(2,1)S(1)}, bf16[3072,152]{0,1:T(8,128)(2,1)}) fusion(f32[3072,152]{0,1:T(8,128)} %get-tuple-element.47, f32[3072]{0:T(1024)S(1)} %get-tuple-element.46, pred[152]{0:T(512)(128)(4,1)S(1)} %broadcast_compare_fusion.1, f32[3072,152]{0,1:T(8,128)} %get-tuple-element.49, ...), kind=kLoop, calls=%fused_computation.24 | loop fusion | flops 3729408 | bytes 5652632 | tf_op jit(solution)/shard_map/reduce_sum | solution.py:37
  78.5 2.5 copy.100
  81.0 1.6 copy.99
  82.5 3.3 %fusion.38 = f32[32,2,48,128]{3,2,1,0:T(8,128)} fusion(bf16[32,2,48,152]{3,2,1,0:T(8,128)(2,1)} %bitcast.166, bf16[1,152,256]{2,1,0:T(8,128)(2,1)S(1)} %get-tuple-element.32), kind=kOutput, calls=%fused_computation.74 | convolution fusion | flops 119537664 | bytes 2545664 | tf_op jit(solution)/shard_map/dot_general | solution.py:39
  85.8 1.7 fusion.39
  87.7 3.7 %fusion.5 = (f32[3072]{0:T(1024)S(1)}, f32[3072]{0:T(1024)S(1)}, bf16[3072,152]{0,1:T(8,128)(2,1)S(1)}, bf16[3072,152]{0,1:T(8,128)(2,1)}) fusion(f32[3072,152]{0,1:T(8,128)} %get-tuple-element.43, f32[3072]{0:T(1024)S(1)} %get-tuple-element.42, pred[152]{0:T(512)(128)(4,1)S(1)} %iota_compare_fusion.2, f32[3072,152]{0,1:T(8,128)} %get-tuple-element.45, ...), kind=kLoop, calls=%fused_computation.20 | loop fusion | flops 3729408 | bytes 5652632 | tf_op jit(solution)/shard_map/reduce_sum | solution.py:37
  91.4 2.5 copy.97
  93.9 1.5 copy.96
  96.1 0.8 reshape.496
  96.8 9.2 %all-to-all-start.2 = ((f32[32,1,192]{2,1,0:T(1,128)}), f32[32,1,192]{2,1,0:T(1,128)S(1)}, u32[]{:S(2)}, u32[]{:S(2)}) async-start(f32[32,1,192]{2,1,0:T(1,128)} %reshape.496), calls=%async_computation.2 | async-start | bytes 65536 | tf_op jit(solution)/shard_map/all_to_all | solution.py:110
  106.1 3.3 %fusion.40 = f32[32,2,48,128]{3,2,1,0:T(8,128)} fusion(bf16[32,2,48,152]{3,2,1,0:T(8,128)(2,1)} %bitcast.164, bf16[1,152,256]{2,1,0:T(8,128)(2,1)S(1)} %get-tuple-element.34), kind=kOutput, calls=%fused_computation.80 | convolution fusion | flops 119537664 | bytes 2545664 | tf_op jit(solution)/shard_map/dot_general | solution.py:39
  109.4 1.7 fusion.41
  111.1 1.7 copy.98
  112.8 8.1 %mul.105 = f32[3072,2,128]{2,1,0:T(2,128)} broadcast(f32[3072,2]{1,0:T(8,128)} %copy.98), dimensions={0,1} | broadcast | bytes 3170304 | tf_op jit(solution)/shard_map/mul | solution.py:63
  120.9 5.5 %mul.106 = f32[32,2,48,256]{3,2,1,0:T(8,128)} reshape(f32[3072,2,128]{2,1,0:T(2,128)} %mul.105) | data formatting | bytes 6291456 | tf_op jit(solution)/shard_map/mul | solution.py:63
  126.4 1.7 copy.101
  128.1 8.1 %mul.108 = f32[3072,2,128]{2,1,0:T(2,128)} broadcast(f32[3072,2]{1,0:T(8,128)} %copy.101), dimensions={0,1} | broadcast | bytes 3170304 | tf_op jit(solution)/shard_map/mul | solution.py:64
  136.2 5.5 %mul.109 = f32[32,2,48,256]{3,2,1,0:T(8,128)} reshape(f32[3072,2,128]{2,1,0:T(2,128)} %mul.108) | data formatting | bytes 6291456 | tf_op jit(solution)/shard_map/mul | solution.py:64
  141.8 0.8 reshape.498
  142.6 9.1 %all-to-all-start.3 = ((f32[32,1,192]{2,1,0:T(1,128)}), f32[32,1,192]{2,1,0:T(1,128)S(1)}, u32[]{:S(2)}, u32[]{:S(2)}) async-start(f32[32,1,192]{2,1,0:T(1,128)} %reshape.498), calls=%async_computation.3 | async-start | bytes 65536 | tf_op jit(solution)/shard_map/all_to_all | solution.py:117
  151.6 7.4 %fusion.4 = f32[32,2,48,256]{3,2,1,0:T(8,128)} fusion(f32[32,2,48,256]{3,2,1,0:T(8,128)} %mul.106, f32[32,2,48,128]{3,2,1,0:T(8,128)} %fusion.40, f32[32,2,48,128]{3,2,1,0:T(8,128)} %fusion.41, f32[32,2,48,256]{3,2,1,0:T(8,128)} %mul.109, f32[32,2,48,128]{3,2,1,0:T(8,128)} %fusion.38, f32[32,2,48,128]{3,2,1,0:T(8,128)} %fusion.39), kind=kLoop, calls=%fused_computation.13 | loop fusion | flops 3932160 | bytes 15728640 | tf_op jit(solution)/shard_map/add | solution.py:63
  159.0 1.4 all-to-all-done.3
  160.4 0.6 copy-done.10
  161.0 8.0 %all-to-all-start.1 = ((f32[32,2,48,256]{3,2,1,0:T(8,128)}), f32[32,2,48,256]{3,2,1,0:T(8,128)}, u32[]{:S(2)}, u32[]{:S(2)}) async-start(f32[32,2,48,256]{3,2,1,0:T(8,128)} %fusion.4), calls=%async_computation.1 | async-start | bytes 6291456 | tf_op jit(solution)/shard_map/all_to_all | solution.py:124
  169.6 1.2 fusion.55
  170.7 1.3 fusion.56
  172.7 0.6 stack.87
  173.3 0.6 stack.88
  174.0 0.7 broadcast_in_dim.103
  174.7 0.6 pad_clamp_fusion.1
  175.9 1.2 fusion.22
  177.1 1.2 fusion.24
  178.9 0.7 reduce.17
  179.8 1.5 reduce.16
  181.3 0.7 reshape.499
  182.1 0.9 copy.120
  182.9 0.7 gather_fusion.2
  183.7 0.7 gather_fusion.3
  184.4 0.8 fusion.46
  185.2 0.9 copy.110
  186.1 0.9 copy.114
  187.0 0.9 copy.121
  187.9 51.7 %all-to-all-done.1 = f32[32,2,48,256]{3,2,1,0:T(8,128)} async-done(((f32[32,2,48,256]{3,2,1,0:T(8,128)}), f32[32,2,48,256]{3,2,1,0:T(8,128)}, u32[]{:S(2)}, u32[]{:S(2)}) %all-to-all-start.1) | async-done | bytes 3145760 | tf_op jit(solution)/shard_map/all_to_all | solution.py:124
  239.6 3.4 %gather_fusion = f32[13,48,256]{2,1,0:T(8,128)} fusion(f32[64,48,256]{2,1,0:T(8,128)} %bitcast.38, s32[1024]{0:T(1024)} %pad_clamp_fusion.1), kind=kCustom, calls=%fused_computation.2 | custom fusion | bytes 1278004 | tf_op jit(solution)/shard_map/jit(_take)/gather | solution.py:135
  243.0 1.8 mul.113
  244.9 1.7 mul.116
  246.6 0.8 div.11
  247.5 1.0 fusion.15
  248.7 1.6 gather_fusion.1
  250.5 0.7 copy.124
  251.2 56.6 %all-gather.2.cloned.1.call-done = bf16[624,4096]{1,0:T(8,128)(2,1)} async-done(((bf16[624,256]{1,0:T(8,128)(2,1)}), bf16[624,4096]{1,0:T(8,128)(2,1)}) %all-gather.2.cloned.1.call-update) | async-done | bytes 5111824 | tf_op jit(solution)/shard_map/all_gather | solution.py:143
  307.8 4.7 %convolution_convert_fusion.1 = bf16[624,256]{1,0:T(8,128)(2,1)} fusion(bf16[624,4096]{1,0:T(8,128)(2,1)} %all-gather.2.cloned.1.call-done, bf16[4096,256]{1,0:T(8,128)(2,1)S(1)} %copy-done), kind=kOutput, calls=%fused_computation.28 | convolution fusion | flops 1308782592 | bytes 7528448 | tf_op jit(solution)/shard_map/dot_general | solution.py:142
  (78 shorter events, 4.2 us)
Async XLA Ops:
  7.2 300.6 %copy-start = (bf16[4096,256]{1,0:T(8,128)(2,1)S(1)}, bf16[4096,256]{1,0:T(8,128)(2,1)}, u32[]{:S(2)}) copy-start(bf16[4096,256]{1,0:T(8,128)(2,1)} %param.21) | copy-start | bytes 6291460
  13.0 10.8 %copy-start.14 = (bf16[1,2,152,256]{3,2,1,0:T(8,128)(2,1)S(1)}, bf16[1,2,152,256]{3,2,1,0:T(8,128)(2,1)}, u32[]{:S(2)}) copy-start(bf16[1,2,152,256]{3,2,1,0:T(8,128)(2,1)} %param.19) | copy-start | bytes 466948
  13.0 17.4 %copy-start.9 = (bf16[1,2,152,256]{3,2,1,0:T(8,128)(2,1)S(1)}, bf16[1,2,152,256]{3,2,1,0:T(8,128)(2,1)}, u32[]{:S(2)}) copy-start(bf16[1,2,152,256]{3,2,1,0:T(8,128)(2,1)} %param.17) | copy-start | bytes 466948
  13.0 49.2 %all-to-all-start = ((bf16[32,2,48,256]{3,2,1,0:T(8,128)(2,1)}), bf16[32,2,48,256]{3,2,1,0:T(8,128)(2,1)}, u32[]{:S(2)}, u32[]{:S(2)}) async-start(bf16[32,2,48,256]{3,2,1,0:T(8,128)(2,1)} %bitcast.162), calls=%async_computation | async-start | bytes 3145728 | tf_op jit(solution)/shard_map/all_to_all | solution.py:99
  23.8 38.4 %collective-permute-start.1 = (bf16[1,2,152,256]{3,2,1,0:T(8,128)(2,1)S(1)}, bf16[1,2,152,256]{3,2,1,0:T(8,128)(2,1)S(1)}, u32[]{:S(2)}, u32[]{:S(2)}) collective-permute-start(bf16[1,2,152,256]{3,2,1,0:T(8,128)(2,1)S(1)} %copy-done.14), channel_id=1, source_target_pairs={{0,16},{16,0},{32,48},{48,32},{64,80},{80,64},{96,112},{112,96},{1... | collective-permute-start | bytes 466952 | tf_op jit(solution)/shard_map/ppermute | solution.py:16
  27.5 34.7 %collective-permute-start = (bf16[152]{0:T(256)(128)(2,1)S(1)}, bf16[152]{0:T(256)(128)(2,1)S(1)}, u32[]{:S(2)}, u32[]{:S(2)}) collective-permute-start(bf16[152]{0:T(256)(128)(2,1)S(1)} %compare_convert_fusion), channel_id=1, source_target_pairs={{0,16},{16,0},{32,48},{48,32},{64,80},{80,64},{96,112},{112,96},{1... | collective-permute-start | bytes 920 | tf_op jit(solution)/shard_map/ppermute | solution.py:16
  82.5 3.3 %copy-start.2 = (bf16[3072,152]{1,0:T(8,128)(2,1)S(1)}, bf16[3072,152]{1,0:T(8,128)(2,1)}, u32[]{:S(2)}) copy-start(bf16[3072,152]{1,0:T(8,128)(2,1)} %copy.99) | copy-start | bytes 2801668
  96.8 45.7 %all-to-all-start.2 = ((f32[32,1,192]{2,1,0:T(1,128)}), f32[32,1,192]{2,1,0:T(1,128)S(1)}, u32[]{:S(2)}, u32[]{:S(2)}) async-start(f32[32,1,192]{2,1,0:T(1,128)} %reshape.496), calls=%async_computation.2 | async-start | bytes 65536 | tf_op jit(solution)/shard_map/all_to_all | solution.py:110
  106.1 3.4 %copy-start.1 = (bf16[3072,152]{1,0:T(8,128)(2,1)S(1)}, bf16[3072,152]{1,0:T(8,128)(2,1)}, u32[]{:S(2)}) copy-start(bf16[3072,152]{1,0:T(8,128)(2,1)} %copy.96) | copy-start | bytes 2801668
  142.6 17.8 %all-to-all-start.3 = ((f32[32,1,192]{2,1,0:T(1,128)}), f32[32,1,192]{2,1,0:T(1,128)S(1)}, u32[]{:S(2)}, u32[]{:S(2)}) async-start(f32[32,1,192]{2,1,0:T(1,128)} %reshape.498), calls=%async_computation.3 | async-start | bytes 65536 | tf_op jit(solution)/shard_map/all_to_all | solution.py:117
  159.0 10.2 %copy-start.8 = (s32[13,48,48]{2,1,0:T(8,128)S(1)}, s32[13,48,48]{2,1,0:T(8,128)}, u32[]{:S(2)}) copy-start(s32[13,48,48]{2,1,0:T(8,128)} %param.14) | copy-start | bytes 359428
  159.0 10.5 %copy-start.3 = (bf16[13,2,48,256]{3,2,1,0:T(8,128)(2,1)S(1)}, bf16[13,2,48,256]{3,2,1,0:T(8,128)(2,1)}, u32[]{:S(2)}) copy-start(bf16[13,2,48,256]{3,2,1,0:T(8,128)(2,1)} %param.13) | copy-start | bytes 1916932
  160.4 0.6 copy-start.10
  161.0 78.6 %all-to-all-start.1 = ((f32[32,2,48,256]{3,2,1,0:T(8,128)}), f32[32,2,48,256]{3,2,1,0:T(8,128)}, u32[]{:S(2)}, u32[]{:S(2)}) async-start(f32[32,2,48,256]{3,2,1,0:T(8,128)} %fusion.4), calls=%async_computation.1 | async-start | bytes 6291456 | tf_op jit(solution)/shard_map/all_to_all | solution.py:124
  169.0 138.8 %all-gather.2.cloned.1.call-start = ((), (), s32[]{:S(2)}) async-start(), calls=%async_computation.4 | async-start | bytes 5431296 | tf_op jit(solution)/shard_map/all_gather | solution.py:143
  169.5 4.4 %copy-start.13 = (s32[13,1]{0,1:T(1,128)S(1)}, s32[13,1]{0,1:T(1,128)}, u32[]{:S(2)}) copy-start(s32[13,1]{0,1:T(1,128)} %param.15) | copy-start | bytes 160
  170.7 1.5 copy-start.5
  172.0 0.7 copy-start.6
  239.6 7.9 %copy-start.12 = (pred[624]{0:T(1024)(128)(4,1)S(1)}, pred[624]{0:T(1024)(128)(4,1)}, u32[]{:S(2)}) copy-start(pred[624]{0:T(1024)(128)(4,1)} %broadcast_in_dim.103) | copy-start | bytes 1876
  243.0 3.6 %copy-start.7 = (f32[13,48,2]{2,1,0:T(8,128)S(1)}, f32[13,48,2]{2,1,0:T(8,128)}, u32[]{:S(2)}) copy-start(f32[13,48,2]{2,1,0:T(8,128)} %copy.121) | copy-start | bytes 14980
  243.0 4.4 %copy-start.4 = (f32[13,48,256]{2,1,0:T(8,128)S(1)}, f32[13,48,256]{2,1,0:T(8,128)}, u32[]{:S(2)}) copy-start(f32[13,48,256]{2,1,0:T(8,128)} %gather_fusion) | copy-start | bytes 1916932
  247.5 1.0 copy-start.11
Sparse Core Ops, SparseCore 0:
  248.6 59.1 all-gather.1
where the time goes:
time: 321 us; the launch traced here: 319 us
  waiting for transfers between devices  141 us (44%)
  local copies, waits for them, and re-layouts  63.3 us (20%)
  starting transfers between devices  42.5 us (13%)
  matrix products  33.4 us (10%)
  other arithmetic  22.8 us (7%)
  between operations  15.8 us (5%)
    all_gather x1, waiting for transfers between devices, local(): lax.all_gather(attn, 'tp', axis=1, tiled=True)  56.6 us
    all_to_all x1, waiting for transfers between devices, local(): lax.all_to_all(merged_accum.reshape(groups, per_group, TREE, local_cols),...  51.7 us
    ppermute x2, waiting for transfers between devices, swapped(): return lax.ppermute(value, axis, pairs)  31.8 us
    mul x3, local copies, waits for them, and re-layouts, combine_parts(): accum_first.reshape(split_shape) * factor_first[..., None]  15.5 us
    mul x3, local copies, waits for them, and re-layouts, combine_parts(): accum_second.reshape(split_shape) * factor_second[..., None]  15.4 us
    dot_general x6, matrix products, attend_part(): lax.dot_general(query_rows[:, :, lower:upper], key_rows[:, :, lower:upper...  14.7 us
    dot_general x6, matrix products, attend_part(): lax.dot_general(raw_weights.astype(jnp.bfloat16), value_rows[:, :, lower:...  12.4 us
    all_to_all x1, starting transfers between devices, local(): lax.all_to_all(outbound, 'rep', split_axis=0, concat_axis=0, tiled=True)  10.7 us
  transfers between devices with their start and end apart: 7, of which 4 were waited for; matrix products, arithmetic and copies ran while one was open for 20% of the time, Pallas kernels for 0%

commit v1 on v0

--- a/solution.py
+++ b/solution.py
@@ -140,7 +140,9 @@
     attn = final_accum.reshape(req_here, TREE, heads_here, HD) / final_total[..., None]
     attn = attn.reshape(req_here * TREE, local_cols).astype(jnp.bfloat16)
     summed = jnp.dot(
-        lax.all_gather(attn, "tp", axis=1, tiled=True),
+        jnp.concatenate(
+            lax.all_to_all(jnp.stack([attn] * lax.axis_size("tp")), "tp", 0, 0), axis=1
+        ),
         out_weight,
         preferred_element_type=jnp.float32,
     )

time: 321 us -> 387 us (1.21)
  waiting for transfers between devices: 141 us -> 197 us
  starting transfers between devices: 42.5 us -> 57.7 us
  between operations: 15.8 us -> 2.45 us
  local copies, waits for them, and re-layouts: 63.3 us -> 73.7 us
    all_to_all x0 -> x1, waiting for transfers between devices: none -> 111 us  [local(): lax.all_to_all(jnp.stack([attn] * lax.axis_size('tp')), 'tp', 0, 0)]
    all_gather x1 -> x0, waiting for transfers between devices: 56.6 us -> none  [local(): lax.all_gather(attn, 'tp', axis=1, tiled=True)]
    all_to_all x0 -> x1, starting transfers between devices: none -> 15.4 us  [local(): lax.all_to_all(jnp.stack([attn] * lax.axis_size('tp')), 'tp', 0, 0)]
    reshape x0 -> x1, local copies, waits for them, and re-layouts: none -> 7.8 us  [local(): jnp.concatenate(lax.all_to_all(jnp.stack([attn] * lax.axis_size('tp')), '...]
  transfers between devices with their start and end apart: 7 -> 7, of which waited for: 4 -> 4; matrix products, arithmetic and copies ran while one was open for 20% -> 16% of each run, Pallas kernels for 0% -> 0%
where the time goes in v1:
time: 387 us; the launch traced here: 385 us
  waiting for transfers between devices  197 us (51%)
  local copies, waits for them, and re-layouts  73.7 us (19%)
  starting transfers between devices  57.7 us (15%)
  matrix products  32.5 us (8%)
  other arithmetic  22 us (6%)
    all_to_all x1, waiting for transfers between devices, local(): lax.all_to_all(jnp.stack([attn] * lax.axis_size('tp')), 'tp', 0, 0)  111 us
    all_to_all x1, waiting for transfers between devices, local(): lax.all_to_all(merged_accum.reshape(groups, per_group, TREE, local_cols),...  53 us
    ppermute x2, waiting for transfers between devices, swapped(): return lax.ppermute(value, axis, pairs)  31.8 us
    mul x3, local copies, waits for them, and re-layouts, combine_parts(): accum_first.reshape(split_shape) * factor_first[..., None]  15.5 us
    all_to_all x1, starting transfers between devices, local(): lax.all_to_all(jnp.stack([attn] * lax.axis_size('tp')), 'tp', 0, 0)  15.4 us
    mul x3, local copies, waits for them, and re-layouts, combine_parts(): accum_second.reshape(split_shape) * factor_second[..., None]  15.4 us
    dot_general x6, matrix products, attend_part(): lax.dot_general(query_rows[:, :, lower:upper], key_rows[:, :, lower:upper...  13.6 us
    dot_general x6, matrix products, attend_part(): lax.dot_general(raw_weights.astype(jnp.bfloat16), value_rows[:, :, lower:...  12.4 us
  transfers between devices with their start and end apart: 7, of which 4 were waited for; matrix products, arithmetic and copies ran while one was open for 16% of the time, Pallas kernels for 0%

profile of v1, /device:TPU:1, one launch (start us, length us, event | category | flops | bytes accessed | tf_op | source)
XLA Modules:
  0.0 385.0 jit_solution(6946388776180838661)
XLA Ops:
  0.6 1.0 convert_reduce_fusion
  1.6 1.1 compare_and_fusion.1
  2.8 1.7 convolution_convert_fusion
  4.5 2.0 copy.135
  6.5 10.7 %all-to-all-start = ((bf16[32,2,48,256]{3,2,1,0:T(8,128)(2,1)}), bf16[32,2,48,256]{3,2,1,0:T(8,128)(2,1)}, u32[]{:S(2)}, u32[]{:S(2)}) async-start(bf16[32,2,48,256]{3,2,1,0:T(8,128)(2,1)} %bitcast.165), calls=%async_computation | async-start | bytes 3145728 | tf_op jit(solution)/shard_map/all_to_all | solution.py:99
  17.3 3.1 collective-permute-start.1
  21.0 2.2 collective-permute-start
  23.9 31.8 %collective-permute-done = bf16[152]{0:T(256)(128)(2,1)S(1)} collective-permute-done((bf16[152]{0:T(256)(128)(2,1)S(1)}, bf16[152]{0:T(256)(128)(2,1)S(1)}, u32[]{:S(2)}, u32[]{:S(2)}) %collective-permute-start) | collective-permute-done | bytes 336 | tf_op jit(solution)/shard_map/ppermute | solution.py:16
  55.7 3.1 fusion.59
  58.8 3.1 fusion.60
  61.9 3.1 fusion.57
  65.0 3.0 fusion.58
  68.2 3.8 fusion.9
  72.0 2.5 copy.103
  74.4 1.6 copy.102
  76.0 3.3 fusion.38
  79.3 1.7 fusion.39
  81.2 3.7 fusion.5
  84.9 2.5 copy.100
  87.4 1.5 copy.99
  89.5 0.8 reshape.521
  90.3 9.2 %all-to-all-start.2 = ((f32[32,1,192]{2,1,0:T(1,128)}), f32[32,1,192]{2,1,0:T(1,128)S(1)}, u32[]{:S(2)}, u32[]{:S(2)}) async-start(f32[32,1,192]{2,1,0:T(1,128)} %reshape.521), calls=%async_computation.2 | async-start | bytes 65536 | tf_op jit(solution)/shard_map/all_to_all | solution.py:110
  99.5 3.3 fusion.40
  102.9 1.7 fusion.41
  104.6 1.7 copy.101
  106.2 8.1 %mul.109 = f32[3072,2,128]{2,1,0:T(2,128)} broadcast(f32[3072,2]{1,0:T(8,128)} %copy.101), dimensions={0,1} | broadcast | bytes 3170304 | tf_op jit(solution)/shard_map/mul | solution.py:63
  114.4 5.5 %mul.110 = f32[32,2,48,256]{3,2,1,0:T(8,128)} reshape(f32[3072,2,128]{2,1,0:T(2,128)} %mul.109) | data formatting | bytes 6291456 | tf_op jit(solution)/shard_map/mul | solution.py:63
  119.9 1.7 copy.104
  121.6 8.1 %mul.112 = f32[3072,2,128]{2,1,0:T(2,128)} broadcast(f32[3072,2]{1,0:T(8,128)} %copy.104), dimensions={0,1} | broadcast | bytes 3170304 | tf_op jit(solution)/shard_map/mul | solution.py:64
  129.7 5.5 %mul.113 = f32[32,2,48,256]{3,2,1,0:T(8,128)} reshape(f32[3072,2,128]{2,1,0:T(2,128)} %mul.112) | data formatting | bytes 6291456 | tf_op jit(solution)/shard_map/mul | solution.py:64
  135.3 0.8 reshape.523
  136.0 9.1 %all-to-all-start.3 = ((f32[32,1,192]{2,1,0:T(1,128)}), f32[32,1,192]{2,1,0:T(1,128)S(1)}, u32[]{:S(2)}, u32[]{:S(2)}) async-start(f32[32,1,192]{2,1,0:T(1,128)} %reshape.523), calls=%async_computation.3 | async-start | bytes 65536 | tf_op jit(solution)/shard_map/all_to_all | solution.py:117
  145.1 7.4 %fusion.4 = f32[32,2,48,256]{3,2,1,0:T(8,128)} fusion(f32[32,2,48,256]{3,2,1,0:T(8,128)} %mul.110, f32[32,2,48,128]{3,2,1,0:T(8,128)} %fusion.40, f32[32,2,48,128]{3,2,1,0:T(8,128)} %fusion.41, f32[32,2,48,256]{3,2,1,0:T(8,128)} %mul.113, f32[32,2,48,128]{3,2,1,0:T(8,128)} %fusion.38, f32[32,2,48,128]{3,2,1,0:T(8,128)} %fusion.39), kind=kLoop, calls=%fused_computation.13 | loop fusion | flops 3932160 | bytes 15728640 | tf_op jit(solution)/shard_map/add | solution.py:63
  152.5 1.4 all-to-all-done.3
  153.9 0.6 copy-done.11
  154.5 8.0 %all-to-all-start.1 = ((f32[32,2,48,256]{3,2,1,0:T(8,128)}), f32[32,2,48,256]{3,2,1,0:T(8,128)}, u32[]{:S(2)}, u32[]{:S(2)}) async-start(f32[32,2,48,256]{3,2,1,0:T(8,128)} %fusion.4), calls=%async_computation.1 | async-start | bytes 6291456 | tf_op jit(solution)/shard_map/all_to_all | solution.py:124
  162.8 1.1 fusion.55
  164.9 0.6 stack.106
  165.5 0.6 stack.107
  166.2 0.7 broadcast_in_dim.103
  168.1 1.2 fusion.22
  169.3 1.2 fusion.24
  171.1 0.7 reduce.17
  172.0 1.5 reduce.16
  173.5 0.7 reshape.524
  174.2 0.9 copy.123
  175.1 0.7 gather_fusion.2
  175.8 0.7 gather_fusion.3
  176.5 0.8 fusion.46
  177.4 0.9 copy.113
  178.3 0.9 copy.117
  179.2 0.9 copy.124
  180.1 53.0 %all-to-all-done.1 = f32[32,2,48,256]{3,2,1,0:T(8,128)} async-done(((f32[32,2,48,256]{3,2,1,0:T(8,128)}), f32[32,2,48,256]{3,2,1,0:T(8,128)}, u32[]{:S(2)}, u32[]{:S(2)}) %all-to-all-start.1) | async-done | bytes 3145760 | tf_op jit(solution)/shard_map/all_to_all | solution.py:124
  233.1 3.4 gather_fusion
  236.5 1.8 mul.117
  238.3 1.7 mul.120
  240.1 0.8 div.13
  241.2 2.6 stack.109
  243.8 15.4 %all-to-all-start.4 = ((bf16[16,624,256]{2,1,0:T(8,128)(2,1)}), bf16[16,624,256]{2,1,0:T(8,128)(2,1)}, u32[]{:S(2)}, u32[]{:S(2)}) async-start(bf16[16,624,256]{2,1,0:T(8,128)(2,1)} %stack.109), calls=%async_computation.4 | async-start | bytes 10223616 | tf_op jit(solution)/shard_map/all_to_all | solution.py:144
  259.4 1.6 gather_fusion.1
  261.3 0.7 copy.128
  261.9 110.5 %all-to-all-done.4 = bf16[16,624,256]{2,1,0:T(8,128)(2,1)} async-done(((bf16[16,624,256]{2,1,0:T(8,128)(2,1)}), bf16[16,624,256]{2,1,0:T(8,128)(2,1)}, u32[]{:S(2)}, u32[]{:S(2)}) %all-to-all-start.4) | async-done | bytes 5111840 | tf_op jit(solution)/shard_map/all_to_all | solution.py:144
  372.4 7.8 %copy.125 = bf16[624,16,256]{0,2,1:T(8,128)(2,1)} copy(bf16[624,16,256]{2,0,1:T(8,128)(2,1)} %bitcast.46) | data formatting | bytes 10223616 | tf_op jit(solution)/shard_map/reshape | solution.py:143
  380.3 4.8 %convolution_convert_fusion.1 = bf16[624,256]{1,0:T(8,128)(2,1)} fusion(bf16[624,4096]{0,1:T(8,128)(2,1)} %bitcast.164, bf16[4096,256]{1,0:T(8,128)(2,1)S(1)} %copy-done), kind=kOutput, calls=%fused_computation.28 | convolution fusion | flops 1308782592 | bytes 7528448 | tf_op jit(solution)/shard_map/dot_general | solution.py:142
  (81 shorter events, 5.0 us)
Async XLA Ops:
  0.6 379.6 %copy-start = (bf16[4096,256]{1,0:T(8,128)(2,1)S(1)}, bf16[4096,256]{1,0:T(8,128)(2,1)}, u32[]{:S(2)}) copy-start(bf16[4096,256]{1,0:T(8,128)(2,1)} %param.21) | copy-start | bytes 6291460
  6.5 10.8 %copy-start.15 = (bf16[1,2,152,256]{3,2,1,0:T(8,128)(2,1)S(1)}, bf16[1,2,152,256]{3,2,1,0:T(8,128)(2,1)}, u32[]{:S(2)}) copy-start(bf16[1,2,152,256]{3,2,1,0:T(8,128)(2,1)} %param.19) | copy-start | bytes 466948
  6.5 17.4 %copy-start.10 = (bf16[1,2,152,256]{3,2,1,0:T(8,128)(2,1)S(1)}, bf16[1,2,152,256]{3,2,1,0:T(8,128)(2,1)}, u32[]{:S(2)}) copy-start(bf16[1,2,152,256]{3,2,1,0:T(8,128)(2,1)} %param.17) | copy-start | bytes 466948
  6.5 49.2 %all-to-all-start = ((bf16[32,2,48,256]{3,2,1,0:T(8,128)(2,1)}), bf16[32,2,48,256]{3,2,1,0:T(8,128)(2,1)}, u32[]{:S(2)}, u32[]{:S(2)}) async-start(bf16[32,2,48,256]{3,2,1,0:T(8,128)(2,1)} %bitcast.165), calls=%async_computation | async-start | bytes 3145728 | tf_op jit(solution)/shard_map/all_to_all | solution.py:99
  17.3 38.4 %collective-permute-start.1 = (bf16[1,2,152,256]{3,2,1,0:T(8,128)(2,1)S(1)}, bf16[1,2,152,256]{3,2,1,0:T(8,128)(2,1)S(1)}, u32[]{:S(2)}, u32[]{:S(2)}) collective-permute-start(bf16[1,2,152,256]{3,2,1,0:T(8,128)(2,1)S(1)} %copy-done.15), channel_id=1, source_target_pairs={{0,16},{16,0},{32,48},{48,32},{64,80},{80,64},{96,112},{112,96},{1... | collective-permute-start | bytes 466952 | tf_op jit(solution)/shard_map/ppermute | solution.py:16
  21.0 34.7 %collective-permute-start = (bf16[152]{0:T(256)(128)(2,1)S(1)}, bf16[152]{0:T(256)(128)(2,1)S(1)}, u32[]{:S(2)}, u32[]{:S(2)}) collective-permute-start(bf16[152]{0:T(256)(128)(2,1)S(1)} %compare_convert_fusion), channel_id=1, source_target_pairs={{0,16},{16,0},{32,48},{48,32},{64,80},{80,64},{96,112},{112,96},{1... | collective-permute-start | bytes 920 | tf_op jit(solution)/shard_map/ppermute | solution.py:16
  76.0 3.3 copy-start.2
  90.3 45.7 %all-to-all-start.2 = ((f32[32,1,192]{2,1,0:T(1,128)}), f32[32,1,192]{2,1,0:T(1,128)S(1)}, u32[]{:S(2)}, u32[]{:S(2)}) async-start(f32[32,1,192]{2,1,0:T(1,128)} %reshape.521), calls=%async_computation.2 | async-start | bytes 65536 | tf_op jit(solution)/shard_map/all_to_all | solution.py:110
  99.5 3.4 copy-start.1
  136.0 17.8 %all-to-all-start.3 = ((f32[32,1,192]{2,1,0:T(1,128)}), f32[32,1,192]{2,1,0:T(1,128)S(1)}, u32[]{:S(2)}, u32[]{:S(2)}) async-start(f32[32,1,192]{2,1,0:T(1,128)} %reshape.523), calls=%async_computation.3 | async-start | bytes 65536 | tf_op jit(solution)/shard_map/all_to_all | solution.py:117
  152.5 10.0 %copy-start.9 = (s32[13,48,48]{2,1,0:T(8,128)S(1)}, s32[13,48,48]{2,1,0:T(8,128)}, u32[]{:S(2)}) copy-start(s32[13,48,48]{2,1,0:T(8,128)} %param.14) | copy-start | bytes 359428
  152.5 10.2 %copy-start.3 = (bf16[13,2,48,256]{3,2,1,0:T(8,128)(2,1)S(1)}, bf16[13,2,48,256]{3,2,1,0:T(8,128)(2,1)}, u32[]{:S(2)}) copy-start(bf16[13,2,48,256]{3,2,1,0:T(8,128)(2,1)} %param.13) | copy-start | bytes 1916932
  153.9 0.6 copy-start.11
  154.5 78.6 %all-to-all-start.1 = ((f32[32,2,48,256]{3,2,1,0:T(8,128)}), f32[32,2,48,256]{3,2,1,0:T(8,128)}, u32[]{:S(2)}, u32[]{:S(2)}) async-start(f32[32,2,48,256]{3,2,1,0:T(8,128)} %fusion.4), calls=%async_computation.1 | async-start | bytes 6291456 | tf_op jit(solution)/shard_map/all_to_all | solution.py:124
  162.6 1.3 copy-start.8
  162.7 3.4 copy-start.14
  163.9 0.7 copy-start.5
  164.2 0.7 copy-start.6
  233.1 7.9 %copy-start.13 = (pred[624]{0:T(1024)(128)(4,1)S(1)}, pred[624]{0:T(1024)(128)(4,1)}, u32[]{:S(2)}) copy-start(pred[624]{0:T(1024)(128)(4,1)} %broadcast_in_dim.103) | copy-start | bytes 1876
  236.5 3.6 copy-start.7
  236.5 4.4 %copy-start.4 = (f32[13,48,256]{2,1,0:T(8,128)S(1)}, f32[13,48,256]{2,1,0:T(8,128)}, u32[]{:S(2)}) copy-start(f32[13,48,256]{2,1,0:T(8,128)} %gather_fusion) | copy-start | bytes 1916932
  243.8 15.4 %copy-start.12 = (s32[13,8]{0,1:T(8,128)S(1)}, s32[13,8]{0,1:T(8,128)}, u32[]{:S(2)}) copy-start(s32[13,8]{0,1:T(8,128)} %param.16) | copy-start | bytes 1252
  243.8 128.6 %all-to-all-start.4 = ((bf16[16,624,256]{2,1,0:T(8,128)(2,1)}), bf16[16,624,256]{2,1,0:T(8,128)(2,1)}, u32[]{:S(2)}, u32[]{:S(2)}) async-start(bf16[16,624,256]{2,1,0:T(8,128)(2,1)} %stack.109), calls=%async_computation.4 | async-start | bytes 10223616 | tf_op jit(solution)/shard_map/all_to_all | solution.py:144
